TPU v7x, 256 devices: a whole 4x4x8 slice. The times are simulated.
256 devices in a mesh: graph: 64 (over x, z, core), rep: 4 (over y).
Axes of the slice: x: 4, y: 4, z: 8, core: 2. Of those that a mesh axis runs over, the one named last changes fastest.
Arguments:
- node_feats: bfloat16 [4, 1024, 49, 256], P('rep', 'graph'), may hold values from -6 to 6
- species: int32 [4, 1024], P('rep', 'graph'), may hold values from 0 to 89
- charge: int32 [4], P('rep'), may hold values from 0 to 8
- species_table: float32 [90, 256], replicated, may hold values from -6 to 6
- charge_table: float32 [9, 256], replicated, may hold values from -6 to 6
- so2_weight: bfloat16 [1792, 1792], replicated, may hold values from -0.125 to 0.125
- edge_frame: bfloat16 [4, 49, 16384], P('rep', None, 'graph'), as said below
- edge_src: int32 [4, 16384], P('rep', 'graph'), may hold values from 0 to 1023, as said below
- edge_dst: int32 [4, 16384], P('rep', 'graph'), may hold values from 0 to 1023, as said below
- edge_count: int32 [4, 64], P('rep', 'graph'), may hold values from 32 to 192, as said below
- out_cotangent: bfloat16 [4, 1024, 49, 256], P('rep', 'graph'), may hold values from -6 to 6
Outputs:
- updated_feats: bfloat16 [4, 1024, 49, 256], P('rep', 'graph')
- feat_grad: bfloat16 [4, 1024, 49, 256], P('rep', 'graph')
- weight_grad: float32 [3211264], P(('graph', 'rep'))
- species_grad: float32 [90, 256], replicated
- charge_grad: float32 [9, 256], replicated
Inputs may be any that keep to these rules, and one draw needn't show every extreme that they name: `edge_count`: live slots of one device per cell. Two devices whose graph indices differ by half the axis hold at most 256 live slots together; in every cell some device holds exactly 192. `edge_src`: in a live slot the source atom's device (index // 16) is at most 2 devices from the slot's device along graph, cyclically; a slot that is not live holds its device's first atom. `edge_dst`: each slot's destination atom belongs to the device that holds the slot; a slot that is not live holds its device's first atom. `edge_frame`: for every edge and degree l the 2l+1 entries of degree l have unit sum of squares; the degree-0 entry is 1.
All inputs are finite; a program needn't handle non-finite values.
Results may differ from a plain program's by a relative error of at most 0.0066.
Values may be sent and summed in bfloat16 or wider, within the bound.
No kernel may reach another device: no remote copies, remote signals or barrier semaphores. Data moves between devices by JAX's collectives and lax.ppermute only.
A program may use at most 128 MiB of HBM per device.

v0:
```python
import jax
import jax.numpy as jnp
from jax import lax
from jax.sharding import PartitionSpec as P

LMAX = 6
SPECIES = 90
CHARGES = 9
REACH = 2
MSG_SCALE = 0.25
PRECISE = lax.Precision.HIGHEST


def from_behind(block, axis, distance):
    devices = range(lax.axis_size(axis))
    route = [((i - distance) % len(devices), i) for i in devices]
    return lax.ppermute(block, axis, route)


def degree_spans():
    return [(degree * degree, (degree + 1) * (degree + 1)) for degree in range(LMAX + 1)]


def gate_forward(pre_act):
    return pre_act * jax.nn.sigmoid(pre_act[:, :1, :])


def gate_backward(pre_act, grad_out):
    sig_gate = jax.nn.sigmoid(pre_act[:, :1, :])
    cross_term = jnp.sum(grad_out * pre_act, axis=1, keepdims=True) * sig_gate * (1.0 - sig_gate)
    scaled = grad_out * sig_gate
    return jnp.concatenate([scaled[:, :1, :] + cross_term, scaled[:, 1:, :]], axis=1)


def gate_rows(pre_act):
    row_count = pre_act.shape[0]
    return gate_forward(pre_act.reshape(row_count, LMAX + 1, -1)).reshape(row_count, -1)


def gate_rows_back(pre_act, grad_out):
    row_count = pre_act.shape[0]
    shaped = gate_backward(
        pre_act.reshape(row_count, LMAX + 1, -1), grad_out.reshape(row_count, LMAX + 1, -1)
    )
    return shaped.reshape(row_count, -1)


def contract_rows(left_mat, right_mat):
    return lax.dot_general(
        left_mat, right_mat, (((0,), (0,)), ((), ())), preferred_element_type=jnp.float32
    )


def edge_coefs(onehot, frame_rows):
    return (onehot[:, :, None] * jnp.transpose(frame_rows)[:, None, :]).reshape(onehot.shape[0], -1)


def local(
    node_feats,
    species,
    charge,
    species_table,
    charge_table,
    so2_weight,
    edge_frame,
    edge_src,
    edge_dst,
    edge_count,
    out_cotangent,
):
    atoms_here = node_feats.shape[1]
    coef_count = node_feats.shape[2]
    channels = node_feats.shape[3]
    edges_here = edge_src.shape[1]
    graph_size = lax.axis_size("graph")
    graph_pos = lax.axis_index("graph")
    live_count = edge_count[0, 0]
    features = node_feats[0].astype(jnp.float32)
    spec_hot = (species[0][:, None] == jnp.arange(SPECIES, dtype=jnp.int32)[None, :]).astype(
        jnp.float32
    )
    charge_hot = (jnp.arange(CHARGES, dtype=jnp.int32) == charge[0]).astype(jnp.float32)
    embedding = (
        jnp.dot(spec_hot, species_table, precision=PRECISE)
        + jnp.dot(charge_hot, charge_table, precision=PRECISE)[None, :]
    )
    hidden = jnp.concatenate(
        [features[:, :1, :] + embedding[:, None, :], features[:, 1:, :]], axis=1
    ).astype(jnp.bfloat16)
    blocks = []
    for offset in range(-REACH, REACH + 1):
        if offset == 0:
            blocks.append(hidden)
        else:
            blocks.append(from_behind(hidden, "graph", -offset))
    block_total = len(blocks)
    nearby = jnp.stack(blocks, axis=0).reshape(block_total * atoms_here, coef_count, channels)
    sources = edge_src[0]
    targets = edge_dst[0]
    slot_ids = jnp.arange(edges_here, dtype=jnp.int32)
    live_mask = slot_ids < live_count
    rel_owner = (sources // atoms_here - graph_pos + REACH) % graph_size
    local_src = rel_owner * atoms_here + sources % atoms_here
    src_hot = (
        (local_src[:, None] == jnp.arange(block_total * atoms_here, dtype=jnp.int32)[None, :])
        & live_mask[:, None]
    ).astype(jnp.bfloat16)
    local_dst = targets - graph_pos * atoms_here
    dst_hot = (
        (local_dst[:, None] == jnp.arange(atoms_here, dtype=jnp.int32)[None, :])
        & live_mask[:, None]
    ).astype(jnp.bfloat16)
    frame_all = edge_frame[0]
    src_coefs = []
    dst_coefs = []
    rotated_pieces = []
    for lower_k, upper_k in degree_spans():
        frame_rows = frame_all[lower_k:upper_k]
        src_coef = edge_coefs(src_hot, frame_rows)
        src_coefs.append(src_coef)
        dst_coefs.append(edge_coefs(dst_hot, frame_rows))
        node_piece = nearby[:, lower_k:upper_k, :].reshape(-1, channels)
        rotated_pieces.append(jnp.dot(src_coef, node_piece, preferred_element_type=jnp.float32))
    rotated = jnp.concatenate(rotated_pieces, axis=1).astype(jnp.bfloat16)
    pre_act = jnp.dot(rotated, so2_weight, preferred_element_type=jnp.float32)
    gated = gate_rows(pre_act).astype(jnp.bfloat16)
    agg_pieces = []
    grad_pieces = []
    cotangent = out_cotangent[0]
    for degree, (lower_k, upper_k) in enumerate(degree_spans()):
        value_piece = gated[:, degree * channels : (degree + 1) * channels]
        agg_pieces.append(
            contract_rows(dst_coefs[degree], value_piece).reshape(
                atoms_here, upper_k - lower_k, channels
            )
        )
        cot_piece = cotangent[:, lower_k:upper_k, :].reshape(-1, channels)
        grad_pieces.append(
            MSG_SCALE * jnp.dot(dst_coefs[degree], cot_piece, preferred_element_type=jnp.float32)
        )
    aggregate = jnp.concatenate(agg_pieces, axis=1)
    updated = (features + MSG_SCALE * aggregate).astype(jnp.bfloat16)
    grad_values = jnp.concatenate(grad_pieces, axis=1)
    grad_pre = gate_rows_back(pre_act, grad_values).astype(jnp.bfloat16)
    weight_part = contract_rows(rotated, grad_pre)
    work_rot = lax.dot_general(
        grad_pre, so2_weight, (((1,), (1,)), ((), ())), preferred_element_type=jnp.float32
    ).astype(jnp.bfloat16)
    node_pieces = []
    for degree, (lower_k, upper_k) in enumerate(degree_spans()):
        rot_piece = work_rot[:, degree * channels : (degree + 1) * channels]
        node_pieces.append(
            contract_rows(src_coefs[degree], rot_piece).reshape(
                block_total * atoms_here, upper_k - lower_k, channels
            )
        )
    node_terms = (
        jnp.concatenate(node_pieces, axis=1)
        .astype(jnp.bfloat16)
        .reshape(block_total, atoms_here, coef_count, channels)
    )
    grad_total = jnp.zeros((atoms_here, coef_count, channels), jnp.float32)
    for offset in range(-REACH, REACH + 1):
        grad_piece = node_terms[offset + REACH]
        if offset == 0:
            grad_total = grad_total + grad_piece.astype(jnp.float32)
        else:
            grad_total = grad_total + from_behind(grad_piece, "graph", offset).astype(jnp.float32)
    feat_grad = (cotangent.astype(jnp.float32) + grad_total).astype(jnp.bfloat16)
    invariant = grad_total[:, 0, :]
    species_part = jnp.dot(jnp.transpose(spec_hot), invariant, precision=PRECISE)
    charge_part = charge_hot[:, None] * jnp.sum(invariant, axis=0)[None, :]
    species_grad, charge_grad = lax.psum((species_part, charge_part), ("graph", "rep"))
    flat_grad = weight_part.reshape(-1)
    weight_grad = lax.psum_scatter(flat_grad, ("graph", "rep"), scatter_dimension=0, tiled=True)
    return (updated[None], feat_grad[None], weight_grad, species_grad, charge_grad)


def solution(mesh):
    in_specs = (
        P("rep", "graph", None, None),
        P("rep", "graph"),
        P("rep"),
        P(),
        P(),
        P(),
        P("rep", None, "graph"),
        P("rep", "graph"),
        P("rep", "graph"),
        P("rep", "graph"),
        P("rep", "graph", None, None),
    )
    out_specs = (
        P("rep", "graph", None, None),
        P("rep", "graph", None, None),
        P(("graph", "rep")),
        P(),
        P(),
    )
    return jax.shard_map(local, mesh=mesh, in_specs=in_specs, out_specs=out_specs, check_vma=False)
```

profile of v0, /device:TPU:8, one launch (start us, length us, event | category | flops | bytes accessed | tf_op | source)
XLA Modules:
  0.0 389.3 jit_solution(1866182456010812411)
XLA Ops:
  8.0 1.1 convert_bitcast_fusion
  11.0 8.1 %collective-permute-start.3 = (bf16[16,49,256]{2,0,1:T(8,128)(2,1)}, bf16[16,49,256]{2,0,1:T(8,128)(2,1)}, u32[]{:S(2)}, u32[]{:S(2)}) collective-permute-start(bf16[16,49,256]{2,0,1:T(8,128)(2,1)} %pad_maximum_fusion.1), channel_id=1, source_target_pairs={{8,0},{12,4},{16,8},{20,12},{24,16},{28,20},{32,24},{36,28},{40,32... | collective-permute-start | bytes 1204232 | tf_op jit(solution)/shard_map/ppermute | solution.py:17
  27.0 1.0 dot_general.204
  28.3 1.0 dot_general.201
  29.5 1.0 dot_general.198
  32.2 1.1 fusion.7
  33.4 1.1 fusion.9
  34.5 1.1 fusion.11
  35.6 1.3 copy-done.3
  36.9 1.0 bitcast_dynamic-update-slice_fusion.3
  38.0 1.2 bitcast_dynamic-update-slice_fusion.2
  39.2 1.2 bitcast_dynamic-update-slice_fusion.1
  40.4 1.0 bitcast_dynamic-update-slice_fusion
  44.2 3.1 fusion.131
  47.3 2.9 copy.52
  50.2 1.0 fusion.85
  51.3 2.5 multiply_reduce_fusion
  53.9 1.0 fusion.58
  55.1 1.9 convolution_convert_fusion
  59.0 1.2 fusion.130
  60.2 4.7 %collective-permute-start.4 = (bf16[16,49,256]{2,0,1:T(8,128)(2,1)}, bf16[16,49,256]{2,0,1:T(8,128)(2,1)}, u32[]{:S(2)}, u32[]{:S(2)}) collective-permute-start(bf16[16,49,256]{2,0,1:T(8,128)(2,1)} %get-tuple-element.9), channel_id=1, source_target_pairs={{8,0},{12,4},{16,8},{20,12},{24,16},{28,20},{32,24},{36,28},{40,32... | collective-permute-start | bytes 1204232 | tf_op jit(solution)/shard_map/ppermute | solution.py:17
  65.1 4.8 %collective-permute-start.5 = (bf16[16,49,256]{2,0,1:T(8,128)(2,1)}, bf16[16,49,256]{2,0,1:T(8,128)(2,1)}, u32[]{:S(2)}, u32[]{:S(2)}) collective-permute-start(bf16[16,49,256]{2,0,1:T(8,128)(2,1)} %get-tuple-element.12), channel_id=1, source_target_pairs={{4,0},{8,4},{12,8},{16,12},{20,16},{24,20},{28,24},{32,28},{36,32}... | collective-permute-start | bytes 1204232 | tf_op jit(solution)/shard_map/ppermute | solution.py:17
  69.9 6.5 %fusion.132 = f32[1792,1792]{1,0:T(8,128)} fusion(bf16[256,1792]{0,1:T(8,128)(2,1)S(1)} %fusion.28, bf16[256,1792]{0,1:T(8,128)(2,1)S(1)} %bitcast.274), kind=kOutput, calls=%fused_computation.227 | convolution fusion | flops 1644167168 | bytes 14680064 | tf_op jit(solution)/shard_map/dot_general | solution.py:49
  76.5 13.6 %reshape.520 = f32[3211264]{0:T(1024)} reshape(f32[1792,1792]{1,0:T(8,128)} %fusion.132) | data formatting | bytes 25690112 | tf_op jit(solution)/shard_map/reshape | solution.py:174
  90.1 2.4 fusion.51
  95.9 1.4 mul.342
  97.2 2.9 copy.53
  100.2 2.2 multiply_convert_fusion
  105.3 72.7 %psum.15 = f32[9,256]{1,0:T(8,128)} all-reduce(f32[9,256]{1,0:T(8,128)S(1)} %broadcast_multiply_fusion.16), channel_id=1, replica_groups=mesh['graph'=64,'rep'=4] {'graph','rep'}, use_global_device_ids=true, to_apply=%region_4.5 | all-reduce | flops 2304 | bytes 18432 | tf_op jit(solution)/shard_map/psum | solution.py:173
  178.0 201.4 %all-reduce.4.cloned.1.call-done = (f32[3211264]{0:T(1024)}, f32[90,256]{1,0:T(8,128)}) async-done(((f32[3211264]{0:T(1024)}, f32[90,256]{1,0:T(8,128)}), (f32[3211264]{0:T(1024)}, f32[90,256]{1,0:T(8,128)})) %all-reduce.4.cloned.1.call-update) | async-done | bytes 12937232
  379.4 1.5 dynamic-slice
  381.0 1.5 copy.152
  (183 shorter events, 22.3 us)
Async XLA Ops:
  7.2 2.8 copy-start
  7.2 2.8 copy-start.30
  7.2 13.1 %copy-start.25 = (bf16[1,49,256]{2,1,0:T(8,128)(2,1)S(1)}, bf16[1,49,256]{2,1,0:T(8,128)(2,1)}, u32[]{:S(2)}) copy-start(bf16[1,49,256]{2,1,0:T(8,128)(2,1)} %param.17) | copy-start | bytes 75268
  7.2 13.2 %copy-start.4 = (bf16[1,16,49,256]{3,1,2,0:T(8,128)(2,1)S(1)}, bf16[1,16,49,256]{3,1,2,0:T(8,128)(2,1)}, u32[]{:S(2)}) copy-start(bf16[1,16,49,256]{3,1,2,0:T(8,128)(2,1)} %param.21) | copy-start | bytes 1204228
  7.2 15.7 %copy-start.32 = (s32[1,256]{1,0:T(1,128)S(1)}, s32[1,256]{1,0:T(1,128)}, u32[]{:S(2)}) copy-start(s32[1,256]{1,0:T(1,128)} %param.18) | copy-start | bytes 3076
  7.2 15.8 %copy-start.33 = (s32[1,256]{1,0:T(1,128)S(1)}, s32[1,256]{1,0:T(1,128)}, u32[]{:S(2)}) copy-start(s32[1,256]{1,0:T(1,128)} %param.19) | copy-start | bytes 3076
  7.2 372.2 %all-reduce.4.cloned.1.call-start = ((), (), s32[]{:S(2)}) async-start(), calls=%async_computation | async-start | bytes 25886720
  11.0 29.3 %collective-permute-start.3 = (bf16[16,49,256]{2,0,1:T(8,128)(2,1)}, bf16[16,49,256]{2,0,1:T(8,128)(2,1)}, u32[]{:S(2)}, u32[]{:S(2)}) collective-permute-start(bf16[16,49,256]{2,0,1:T(8,128)(2,1)} %pad_maximum_fusion.1), channel_id=1, source_target_pairs={{8,0},{12,4},{16,8},{20,12},{24,16},{28,20},{32,24},{36,28},{40,32... | collective-permute-start | bytes 1204232 | tf_op jit(solution)/shard_map/ppermute | solution.py:17
  19.1 20.1 %collective-permute-start.2 = (bf16[16,49,256]{2,0,1:T(8,128)(2,1)}, bf16[16,49,256]{2,0,1:T(8,128)(2,1)}, u32[]{:S(2)}, u32[]{:S(2)}) collective-permute-start(bf16[16,49,256]{2,0,1:T(8,128)(2,1)} %pad_maximum_fusion.1), channel_id=1, source_target_pairs={{4,0},{8,4},{12,8},{16,12},{20,16},{24,20},{28,24},{32,28},{36,32}... | collective-permute-start | bytes 1204232 | tf_op jit(solution)/shard_map/ppermute | solution.py:17
  19.2 18.7 %collective-permute-start.1 = (bf16[16,49,256]{2,0,1:T(8,128)(2,1)}, bf16[16,49,256]{2,0,1:T(8,128)(2,1)}, u32[]{:S(2)}, u32[]{:S(2)}) collective-permute-start(bf16[16,49,256]{2,0,1:T(8,128)(2,1)} %pad_maximum_fusion.1), channel_id=1, source_target_pairs={{252,0},{0,4},{4,8},{8,12},{12,16},{16,20},{20,24},{24,28},{28,32}... | collective-permute-start | bytes 1204232 | tf_op jit(solution)/shard_map/ppermute | solution.py:17
  19.6 17.3 %collective-permute-start = (bf16[16,49,256]{2,0,1:T(8,128)(2,1)}, bf16[16,49,256]{2,0,1:T(8,128)(2,1)}, u32[]{:S(2)}, u32[]{:S(2)}) collective-permute-start(bf16[16,49,256]{2,0,1:T(8,128)(2,1)} %pad_maximum_fusion.1), channel_id=1, source_target_pairs={{248,0},{252,4},{0,8},{4,12},{8,16},{12,20},{16,24},{20,28},{24,32... | collective-permute-start | bytes 1204232 | tf_op jit(solution)/shard_map/ppermute | solution.py:17
  20.3 36.7 %copy-start.34 = (bf16[256]{0:T(256)(128)(2,1)}, bf16[256]{0:T(256)(128)(2,1)S(1)}, u32[]{:S(2)}) copy-start(bf16[256]{0:T(256)(128)(2,1)S(1)} %slice_reduce_fusion.1) | copy-start | bytes 1540
  20.4 13.0 %copy-start.23 = (bf16[256,11]{0,1:T(8,128)(2,1)}, bf16[256,11]{0,1:T(8,128)(2,1)S(1)}, u32[]{:S(2)}) copy-start(bf16[256,11]{0,1:T(8,128)(2,1)S(1)} %slice_bitcast_fusion.29) | copy-start | bytes 16900
  23.0 34.0 %copy-start.28 = (pred[256]{0:T(512)(128)(4,1)}, pred[256]{0:T(512)(128)(4,1)S(1)}, u32[]{:S(2)}) copy-start(pred[256]{0:T(512)(128)(4,1)S(1)} %iota_compare_fusion.5) | copy-start | bytes 772
  23.0 7.5 %copy-start.26 = (s32[1,256]{1,0:T(1,128)}, s32[1,256]{1,0:T(1,128)S(1)}, u32[]{:S(2)}) copy-start(s32[1,256]{1,0:T(1,128)S(1)} %broadcast_subtract_fusion) | copy-start | bytes 3076
  23.7 8.0 %copy-start.17 = (bf16[256,16,5]{0,2,1:T(8,128)(2,1)}, bf16[256,16,5]{0,2,1:T(8,128)(2,1)S(1)}, u32[]{:S(2)}) copy-start(bf16[256,16,5]{0,2,1:T(8,128)(2,1)S(1)} %broadcast_multiply_fusion.11) | copy-start | bytes 122884
  23.9 2.9 copy-start.7
  23.9 8.1 %copy-start.15 = (bf16[256,16,7]{0,2,1:T(8,128)(2,1)}, bf16[256,16,7]{0,2,1:T(8,128)(2,1)S(1)}, u32[]{:S(2)}) copy-start(bf16[256,16,7]{0,2,1:T(8,128)(2,1)S(1)} %broadcast_multiply_fusion.10) | copy-start | bytes 172036
  24.0 2.8 copy-start.9
  37.9 6.3 %slice-start = ((s8[6422528]{0:T(1024)(128)(4,1)}), s8[4194304]{0:T(1024)(128)(4,1)S(1)}, s32[]{:S(2)}) async-start(s8[6422528]{0:T(1024)(128)(4,1)} %bitcast.265), calls=%async_computation.1 | async-start | bytes 8388608
  41.4 2.8 slice-start.1
  47.3 7.7 %slice-start.2 = ((s8[6422528]{0:T(1024)(128)(4,1)}), s8[2228224]{0:T(1024)(128)(4,1)S(1)}, s32[]{:S(2)}) async-start(s8[6422528]{0:T(1024)(128)(4,1)} %bitcast.267), calls=%async_computation.3 | async-start | bytes 4456448
  51.2 3.8 slice-start.3
  55.1 2.6 copy-start.19
  60.2 29.9 %collective-permute-start.4 = (bf16[16,49,256]{2,0,1:T(8,128)(2,1)}, bf16[16,49,256]{2,0,1:T(8,128)(2,1)}, u32[]{:S(2)}, u32[]{:S(2)}) collective-permute-start(bf16[16,49,256]{2,0,1:T(8,128)(2,1)} %get-tuple-element.9), channel_id=1, source_target_pairs={{8,0},{12,4},{16,8},{20,12},{24,16},{28,20},{32,24},{36,28},{40,32... | collective-permute-start | bytes 1204232 | tf_op jit(solution)/shard_map/ppermute | solution.py:17
  64.9 25.2 %collective-permute-start.7 = (bf16[16,49,256]{2,0,1:T(8,128)(2,1)}, bf16[16,49,256]{2,0,1:T(8,128)(2,1)}, u32[]{:S(2)}, u32[]{:S(2)}) collective-permute-start(bf16[16,49,256]{2,0,1:T(8,128)(2,1)} %get-tuple-element.10), channel_id=1, source_target_pairs={{248,0},{252,4},{0,8},{4,12},{8,16},{12,20},{16,24},{20,28},{24,32... | collective-permute-start | bytes 1204232 | tf_op jit(solution)/shard_map/ppermute | solution.py:17
  64.9 25.2 %collective-permute-start.6 = (bf16[16,49,256]{2,0,1:T(8,128)(2,1)}, bf16[16,49,256]{2,0,1:T(8,128)(2,1)}, u32[]{:S(2)}, u32[]{:S(2)}) collective-permute-start(bf16[16,49,256]{2,0,1:T(8,128)(2,1)} %get-tuple-element.11), channel_id=1, source_target_pairs={{252,0},{0,4},{4,8},{8,12},{12,16},{16,20},{20,24},{24,28},{28,32}... | collective-permute-start | bytes 1204232 | tf_op jit(solution)/shard_map/ppermute | solution.py:17
  65.1 25.0 %collective-permute-start.5 = (bf16[16,49,256]{2,0,1:T(8,128)(2,1)}, bf16[16,49,256]{2,0,1:T(8,128)(2,1)}, u32[]{:S(2)}, u32[]{:S(2)}) collective-permute-start(bf16[16,49,256]{2,0,1:T(8,128)(2,1)} %get-tuple-element.12), channel_id=1, source_target_pairs={{4,0},{8,4},{12,8},{16,12},{20,16},{24,20},{28,24},{32,28},{36,32}... | collective-permute-start | bytes 1204232 | tf_op jit(solution)/shard_map/ppermute | solution.py:17
  76.5 13.6 %copy-start.5 = (bf16[1,16,49,256]{3,1,2,0:T(8,128)(2,1)S(1)}, bf16[1,16,49,256]{3,1,2,0:T(8,128)(2,1)}, u32[]{:S(2)}) copy-start(bf16[1,16,49,256]{3,1,2,0:T(8,128)(2,1)} %param.21) | copy-start | bytes 1204228
  90.1 3.4 copy-start.31
  97.2 2.9 copy-start.2
  102.4 280.1 %copy-start.1 = (f32[90,256]{1,0:T(8,128)S(1)}, f32[90,256]{1,0:T(8,128)}, u32[]{:S(2)}) copy-start(f32[90,256]{1,0:T(8,128)} %param.14) | copy-start | bytes 276484
  (17 other events, 24.3 us)
Sparse Core Ops, SparseCore 0:
  94.6 284.8 all-reduce.3
where the time goes:
time: 390 us; the launch traced here: 389 us
  waiting for transfers between devices  201 us (52%)
  blocking collectives  72.7 us (19%)
  local copies, waits for them, and re-layouts  42 us (11%)
  matrix products  23.6 us (6%)
  starting transfers between devices  19 us (5%)
  between operations  16.5 us (4%)
  other arithmetic  14.1 us (4%)
    unnamed x2, waiting for transfers between devices  201 us
    psum x1, blocking collectives, local(): lax.psum((species_part, charge_part), ('graph', 'rep'))  72.7 us
    ppermute x8, starting transfers between devices, from_behind(): return lax.ppermute(block, axis, route)  19 us
    reshape x1, local copies, waits for them, and re-layouts, local(): flat_grad = weight_part.reshape(-1)  13.6 us
    unnamed x85, local copies, waits for them, and re-layouts  10.1 us
    dot_general x15, matrix products, contract_rows(): lax.dot_general(left_mat, right_mat, (((0,), (0,)), ((), ())), preferred_...  9.34 us
  transfers between devices with their start and end apart: 9, of which 1 were waited for; matrix products, arithmetic and copies ran while one was open for 12% of the time, Pallas kernels for 0%

commit v1 on v0

--- a/solution.py
+++ b/solution.py
@@ -170,7 +170,7 @@
     invariant = grad_total[:, 0, :]
     species_part = jnp.dot(jnp.transpose(spec_hot), invariant, precision=PRECISE)
     charge_part = charge_hot[:, None] * jnp.sum(invariant, axis=0)[None, :]
-    species_grad, charge_grad = lax.psum((species_part, charge_part), ("graph", "rep"))
+    species_grad, charge_grad = lax.psum(lax.psum((species_part, charge_part), "rep"), "graph")
     flat_grad = weight_part.reshape(-1)
     weight_grad = lax.psum_scatter(flat_grad, ("graph", "rep"), scatter_dimension=0, tiled=True)
     return (updated[None], feat_grad[None], weight_grad, species_grad, charge_grad)

time: 390 us -> 605 us (1.55)
  blocking collectives: 72.7 us -> 262 us
  waiting for transfers between devices: 201 us -> 231 us
    psum x1 -> x2, blocking collectives: 72.7 us -> 262 us  [the longest x1 247 us: local(): lax.psum(lax.psum((species_part, charge_part), 'rep'), 'graph')]
    psum x0 -> x2, waiting for transfers between devices: none -> 182 us  [the longest x1 173 us: local(): lax.psum(lax.psum((species_part, charge_part), 'rep'), 'graph')]
    unnamed x2 -> x4, waiting for transfers between devices: 201 us -> 34.5 us
    ppermute x8, waiting for transfers between devices: 0.02 us -> 14 us  [from_behind(): return lax.ppermute(block, axis, route)]
  transfers between devices with their start and end apart: 9 -> 11, of which waited for: 1 -> 6; matrix products, arithmetic and copies ran while one was open for 12% -> 8% of each run, Pallas kernels for 0% -> 0%
where the time goes in v1:
time: 605 us; the launch traced here: 604 us
  blocking collectives  262 us (43%)
  waiting for transfers between devices  231 us (38%)
  local copies, waits for them, and re-layouts  40 us (7%)
  matrix products  23.6 us (4%)
  starting transfers between devices  19.2 us (3%)
  between operations  16.2 us (3%)
  other arithmetic  12.2 us (2%)
    psum x1, blocking collectives, local(): lax.psum(lax.psum((species_part, charge_part), 'rep'), 'graph')  247 us
    psum x1, waiting for transfers between devices, local(): lax.psum(lax.psum((species_part, charge_part), 'rep'), 'graph')  173 us
    unnamed x4, waiting for transfers between devices  34.5 us
    ppermute x8, starting transfers between devices, from_behind(): return lax.ppermute(block, axis, route)  19.1 us
    psum x1, blocking collectives, local(): lax.psum((species_part, charge_part), 'rep')  14.7 us
    ppermute x8, waiting for transfers between devices, from_behind(): return lax.ppermute(block, axis, route)  14 us
    reshape x1, local copies, waits for them, and re-layouts, local(): flat_grad = weight_part.reshape(-1)  13.5 us
  transfers between devices with their start and end apart: 11, of which 6 were waited for; matrix products, arithmetic and copies ran while one was open for 8% of the time, Pallas kernels for 0%

profile of v1, /device:TPU:8, one launch (start us, length us, event | category | flops | bytes accessed | tf_op | source)
XLA Modules:
  0.0 604.0 jit_solution(12500501064160658863)
XLA Ops:
  8.0 1.1 convert_bitcast_fusion
  11.0 8.1 %collective-permute-start.3 = (bf16[16,49,256]{2,0,1:T(8,128)(2,1)}, bf16[16,49,256]{2,0,1:T(8,128)(2,1)}, u32[]{:S(2)}, u32[]{:S(2)}) collective-permute-start(bf16[16,49,256]{2,0,1:T(8,128)(2,1)} %pad_maximum_fusion.1), channel_id=1, source_target_pairs={{8,0},{12,4},{16,8},{20,12},{24,16},{28,20},{32,24},{36,28},{40,32... | collective-permute-start | bytes 1204232 | tf_op jit(solution)/shard_map/ppermute | solution.py:17
  32.3 1.1 fusion.7
  33.4 1.1 fusion.9
  34.6 1.1 fusion.11
  35.7 1.2 copy-done.5
  38.0 1.2 bitcast_dynamic-update-slice_fusion.2
  39.2 1.2 bitcast_dynamic-update-slice_fusion.1
  40.4 1.0 bitcast_dynamic-update-slice_fusion
  44.3 3.1 fusion.131
  47.4 2.9 copy.52
  51.3 2.5 multiply_reduce_fusion
  53.9 1.0 fusion.58
  55.1 1.9 convolution_convert_fusion
  59.2 4.7 collective-permute-start.4
  64.2 4.8 collective-permute-start.5
  69.1 4.2 collective-permute-done.4
  73.2 6.3 %collective-permute-done.7 = bf16[16,49,256]{2,0,1:T(8,128)(2,1)S(1)} collective-permute-done((bf16[16,49,256]{2,0,1:T(8,128)(2,1)S(1)}, bf16[16,49,256]{2,0,1:T(8,128)(2,1)S(1)}, u32[]{:S(2)}, u32[]{:S(2)}) %collective-permute-start.7) | collective-permute-done | bytes 401440 | tf_op jit(solution)/shard_map/ppermute | solution.py:17
  79.5 3.6 collective-permute-done.6
  83.1 1.1 fusion.51
  85.2 6.5 %fusion.132 = f32[1792,1792]{1,0:T(8,128)} fusion(bf16[256,1792]{0,1:T(8,128)(2,1)S(1)} %fusion.28, bf16[256,1792]{0,1:T(8,128)(2,1)S(1)} %bitcast.274), kind=kOutput, calls=%fused_computation.227 | convolution fusion | flops 1644167168 | bytes 14680064 | tf_op jit(solution)/shard_map/dot_general | solution.py:49
  91.7 13.5 %reshape.520 = f32[3211264]{0:T(1024)} reshape(f32[1792,1792]{1,0:T(8,128)} %fusion.132) | data formatting | bytes 25690112 | tf_op jit(solution)/shard_map/reshape | solution.py:174
  106.7 1.4 mul.342
  108.1 2.9 copy.53
  111.0 1.7 multiply_convert_fusion
  115.6 8.8 %all-reduce.5.cloned.1.call-done = f32[90,256]{1,0:T(8,128)} async-done(((f32[90,256]{1,0:T(8,128)}), f32[90,256]{1,0:T(8,128)}) %all-reduce.5.cloned.1.call-update) | async-done | bytes 92176 | tf_op jit(solution)/shard_map/psum | solution.py:173
  124.4 14.7 %psum.30 = f32[9,256]{1,0:T(8,128)S(1)} all-reduce(f32[9,256]{1,0:T(8,128)S(1)} %broadcast_multiply_fusion.16), channel_id=1, replica_groups=mesh['graph'=64,'rep'=4] {'rep'}, use_global_device_ids=true, to_apply=%region_5.6 | all-reduce | flops 2304 | bytes 18432 | tf_op jit(solution)/shard_map/psum | solution.py:173
  139.1 247.4 %psum.31 = f32[9,256]{1,0:T(8,128)} all-reduce(f32[9,256]{1,0:T(8,128)S(1)} %psum.30), channel_id=1, replica_groups=mesh['graph'=64,'rep'=4] {'graph'}, use_global_device_ids=true, to_apply=%region_6.7 | all-reduce | flops 2304 | bytes 18432 | tf_op jit(solution)/shard_map/psum | solution.py:173
  386.6 34.5 %all-reduce.9.cloned.1.call-done = f32[3211264]{0:T(1024)} async-done(((f32[3211264]{0:T(1024)}), f32[3211264]{0:T(1024)}) %all-reduce.9.cloned.1.call-update) | async-done | bytes 12845072
  421.0 1.5 dynamic-slice
  422.6 173.4 %all-reduce.7.cloned.1.call-done = f32[90,256]{1,0:T(8,128)} async-done(((f32[90,256]{1,0:T(8,128)}), f32[90,256]{1,0:T(8,128)}) %all-reduce.7.cloned.1.call-update) | async-done | bytes 92176 | tf_op jit(solution)/shard_map/psum | solution.py:173
  595.9 1.5 copy.153
  (194 shorter events, 26.7 us)
Async XLA Ops:
  7.2 2.8 copy-start
  7.2 13.1 %copy-start.27 = (bf16[1,49,256]{2,1,0:T(8,128)(2,1)S(1)}, bf16[1,49,256]{2,1,0:T(8,128)(2,1)}, u32[]{:S(2)}) copy-start(bf16[1,49,256]{2,1,0:T(8,128)(2,1)} %param.17) | copy-start | bytes 75268
  7.2 13.2 %copy-start.6 = (bf16[1,16,49,256]{3,1,2,0:T(8,128)(2,1)S(1)}, bf16[1,16,49,256]{3,1,2,0:T(8,128)(2,1)}, u32[]{:S(2)}) copy-start(bf16[1,16,49,256]{3,1,2,0:T(8,128)(2,1)} %param.21) | copy-start | bytes 1204228
  7.2 15.8 %copy-start.34 = (s32[1,256]{1,0:T(1,128)S(1)}, s32[1,256]{1,0:T(1,128)}, u32[]{:S(2)}) copy-start(s32[1,256]{1,0:T(1,128)} %param.18) | copy-start | bytes 3076
  7.2 15.8 %copy-start.35 = (s32[1,256]{1,0:T(1,128)S(1)}, s32[1,256]{1,0:T(1,128)}, u32[]{:S(2)}) copy-start(s32[1,256]{1,0:T(1,128)} %param.19) | copy-start | bytes 3076
  7.2 117.1 %all-reduce.5.cloned.1.call-start = ((), (), s32[]{:S(2)}) async-start(), calls=%async_computation | async-start | bytes 196608 | tf_op jit(solution)/shard_map/psum | solution.py:173
  11.0 29.4 %collective-permute-start.3 = (bf16[16,49,256]{2,0,1:T(8,128)(2,1)}, bf16[16,49,256]{2,0,1:T(8,128)(2,1)}, u32[]{:S(2)}, u32[]{:S(2)}) collective-permute-start(bf16[16,49,256]{2,0,1:T(8,128)(2,1)} %pad_maximum_fusion.1), channel_id=1, source_target_pairs={{8,0},{12,4},{16,8},{20,12},{24,16},{28,20},{32,24},{36,28},{40,32... | collective-permute-start | bytes 1204232 | tf_op jit(solution)/shard_map/ppermute | solution.py:17
  19.1 20.2 %collective-permute-start.2 = (bf16[16,49,256]{2,0,1:T(8,128)(2,1)}, bf16[16,49,256]{2,0,1:T(8,128)(2,1)}, u32[]{:S(2)}, u32[]{:S(2)}) collective-permute-start(bf16[16,49,256]{2,0,1:T(8,128)(2,1)} %pad_maximum_fusion.1), channel_id=1, source_target_pairs={{4,0},{8,4},{12,8},{16,12},{20,16},{24,20},{28,24},{32,28},{36,32}... | collective-permute-start | bytes 1204232 | tf_op jit(solution)/shard_map/ppermute | solution.py:17
  19.2 18.7 %collective-permute-start.1 = (bf16[16,49,256]{2,0,1:T(8,128)(2,1)}, bf16[16,49,256]{2,0,1:T(8,128)(2,1)}, u32[]{:S(2)}, u32[]{:S(2)}) collective-permute-start(bf16[16,49,256]{2,0,1:T(8,128)(2,1)} %pad_maximum_fusion.1), channel_id=1, source_target_pairs={{252,0},{0,4},{4,8},{8,12},{12,16},{16,20},{20,24},{24,28},{28,32}... | collective-permute-start | bytes 1204232 | tf_op jit(solution)/shard_map/ppermute | solution.py:17
  19.6 17.4 %collective-permute-start = (bf16[16,49,256]{2,0,1:T(8,128)(2,1)}, bf16[16,49,256]{2,0,1:T(8,128)(2,1)}, u32[]{:S(2)}, u32[]{:S(2)}) collective-permute-start(bf16[16,49,256]{2,0,1:T(8,128)(2,1)} %pad_maximum_fusion.1), channel_id=1, source_target_pairs={{248,0},{252,4},{0,8},{4,12},{8,16},{12,20},{16,24},{20,28},{24,32... | collective-permute-start | bytes 1204232 | tf_op jit(solution)/shard_map/ppermute | solution.py:17
  20.3 36.8 %copy-start.36 = (bf16[256]{0:T(256)(128)(2,1)}, bf16[256]{0:T(256)(128)(2,1)S(1)}, u32[]{:S(2)}) copy-start(bf16[256]{0:T(256)(128)(2,1)S(1)} %slice_reduce_fusion.1) | copy-start | bytes 1540
  20.4 13.1 %copy-start.25 = (bf16[256,11]{0,1:T(8,128)(2,1)}, bf16[256,11]{0,1:T(8,128)(2,1)S(1)}, u32[]{:S(2)}) copy-start(bf16[256,11]{0,1:T(8,128)(2,1)S(1)} %slice_bitcast_fusion.29) | copy-start | bytes 16900
  23.0 34.1 %copy-start.30 = (pred[256]{0:T(512)(128)(4,1)}, pred[256]{0:T(512)(128)(4,1)S(1)}, u32[]{:S(2)}) copy-start(pred[256]{0:T(512)(128)(4,1)S(1)} %iota_compare_fusion.5) | copy-start | bytes 772
  23.0 7.5 %copy-start.28 = (s32[1,256]{1,0:T(1,128)}, s32[1,256]{1,0:T(1,128)S(1)}, u32[]{:S(2)}) copy-start(s32[1,256]{1,0:T(1,128)S(1)} %broadcast_subtract_fusion) | copy-start | bytes 3076
  23.8 8.0 %copy-start.19 = (bf16[256,16,5]{0,2,1:T(8,128)(2,1)}, bf16[256,16,5]{0,2,1:T(8,128)(2,1)S(1)}, u32[]{:S(2)}) copy-start(bf16[256,16,5]{0,2,1:T(8,128)(2,1)S(1)} %broadcast_multiply_fusion.11) | copy-start | bytes 122884
  23.9 2.9 copy-start.9
  23.9 8.1 %copy-start.17 = (bf16[256,16,7]{0,2,1:T(8,128)(2,1)}, bf16[256,16,7]{0,2,1:T(8,128)(2,1)S(1)}, u32[]{:S(2)}) copy-start(bf16[256,16,7]{0,2,1:T(8,128)(2,1)S(1)} %broadcast_multiply_fusion.10) | copy-start | bytes 172036
  38.0 6.3 %slice-start = ((s8[6422528]{0:T(1024)(128)(4,1)}), s8[4194304]{0:T(1024)(128)(4,1)S(1)}, s32[]{:S(2)}) async-start(s8[6422528]{0:T(1024)(128)(4,1)} %bitcast.265), calls=%async_computation.3 | async-start | bytes 8388608
  47.4 7.7 %slice-start.2 = ((s8[6422528]{0:T(1024)(128)(4,1)}), s8[2228224]{0:T(1024)(128)(4,1)S(1)}, s32[]{:S(2)}) async-start(s8[6422528]{0:T(1024)(128)(4,1)} %bitcast.267), calls=%async_computation.5 | async-start | bytes 4456448
  51.3 3.8 slice-start.3
  58.8 24.3 %copy-start.7 = (bf16[1,16,49,256]{3,1,2,0:T(8,128)(2,1)S(1)}, bf16[1,16,49,256]{3,1,2,0:T(8,128)(2,1)}, u32[]{:S(2)}) copy-start(bf16[1,16,49,256]{3,1,2,0:T(8,128)(2,1)} %param.21) | copy-start | bytes 1204228
  59.2 24.9 %copy-start.33 = (s32[1,16]{1,0:T(1,128)S(1)}, s32[1,16]{1,0:T(1,128)}, u32[]{:S(2)}) copy-start(s32[1,16]{1,0:T(1,128)} %param.12) | copy-start | bytes 196
  59.2 25.9 %copy-start.4 = (bf16[256,7,256]{0,2,1:T(8,128)(2,1)S(1)}, bf16[256,7,256]{0,2,1:T(8,128)(2,1)}, u32[]{:S(2)}) copy-start(bf16[256,7,256]{0,2,1:T(8,128)(2,1)} %copy-done.3) | copy-start | bytes 2752516
  59.2 14.0 %collective-permute-start.4 = (bf16[16,49,256]{2,0,1:T(8,128)(2,1)S(1)}, bf16[16,49,256]{2,0,1:T(8,128)(2,1)S(1)}, u32[]{:S(2)}, u32[]{:S(2)}) collective-permute-start(bf16[16,49,256]{2,0,1:T(8,128)(2,1)S(1)} %get-tuple-element.7), channel_id=1, source_target_pairs={{8,0},{12,4},{16,8},{20,12},{24,16},{28,20},{32,24},{36,28},{40,32... | collective-permute-start | bytes 1204232 | tf_op jit(solution)/shard_map/ppermute | solution.py:17
  64.0 15.5 %collective-permute-start.7 = (bf16[16,49,256]{2,0,1:T(8,128)(2,1)S(1)}, bf16[16,49,256]{2,0,1:T(8,128)(2,1)S(1)}, u32[]{:S(2)}, u32[]{:S(2)}) collective-permute-start(bf16[16,49,256]{2,0,1:T(8,128)(2,1)S(1)} %get-tuple-element.8), channel_id=1, source_target_pairs={{248,0},{252,4},{0,8},{4,12},{8,16},{12,20},{16,24},{20,28},{24,32... | collective-permute-start | bytes 1204232 | tf_op jit(solution)/shard_map/ppermute | solution.py:17
  64.0 19.0 %collective-permute-start.6 = (bf16[16,49,256]{2,0,1:T(8,128)(2,1)S(1)}, bf16[16,49,256]{2,0,1:T(8,128)(2,1)S(1)}, u32[]{:S(2)}, u32[]{:S(2)}) collective-permute-start(bf16[16,49,256]{2,0,1:T(8,128)(2,1)S(1)} %get-tuple-element.9), channel_id=1, source_target_pairs={{252,0},{0,4},{4,8},{8,12},{12,16},{16,20},{20,24},{24,28},{28,32}... | collective-permute-start | bytes 1204232 | tf_op jit(solution)/shard_map/ppermute | solution.py:17
  64.2 18.8 %collective-permute-start.5 = (bf16[16,49,256]{2,0,1:T(8,128)(2,1)S(1)}, bf16[16,49,256]{2,0,1:T(8,128)(2,1)S(1)}, u32[]{:S(2)}, u32[]{:S(2)}) collective-permute-start(bf16[16,49,256]{2,0,1:T(8,128)(2,1)S(1)} %get-tuple-element.10), channel_id=1, source_target_pairs={{4,0},{8,4},{12,8},{16,12},{20,16},{24,20},{28,24},{32,28},{36,32}... | collective-permute-start | bytes 1204232 | tf_op jit(solution)/shard_map/ppermute | solution.py:17
  84.1 7.6 %copy-start.13 = (f32[16,49,256]{2,0,1:T(8,128)}, f32[16,49,256]{2,0,1:T(8,128)S(1)}, u32[]{:S(2)}) copy-start(f32[16,49,256]{2,0,1:T(8,128)S(1)} %get-tuple-element.6) | copy-start | bytes 2408452
  85.1 335.9 %all-reduce.9.cloned.1.call-start = ((), (), s32[]{:S(2)}) async-start(), calls=%async_computation.2 | async-start | bytes 25690112
  105.3 490.6 %all-reduce.7.cloned.1.call-start = ((), (), s32[]{:S(2)}) async-start(), calls=%async_computation.1 | async-start | bytes 196608 | tf_op jit(solution)/shard_map/psum | solution.py:173
  108.1 2.9 copy-start.2
  112.8 484.7 %copy-start.1 = (f32[90,256]{1,0:T(8,128)S(1)}, f32[90,256]{1,0:T(8,128)}, u32[]{:S(2)}) copy-start(f32[90,256]{1,0:T(8,128)} %param.14) | copy-start | bytes 276484
  (21 other events, 34.8 us)
Sparse Core Ops, SparseCore 0:
  85.2 39.0 all-reduce.4
  129.9 291.0 all-reduce.8
  424.5 171.3 all-reduce.6
